TPU v7x, 256 devices: a whole 4x4x8 slice. The times are simulated.
256 devices in a mesh: leaf: 8 (over z), blk: 32 (over x, y, core).
Axes of the slice: x: 4, y: 4, z: 8, core: 2. Of those that a mesh axis runs over, the one named last changes fastest.
Arguments:
- root_sigma: float32 [2, 256, 256], replicated, as said below
- top_inv: bfloat16 [8, 2, 256, 256], P('leaf'), as said below
- top_panels: bfloat16 [8, 2, 256, 256], P('leaf')
- top_parents: int32 [8, 2], P('leaf'), may hold values from 0 to 1
- sub_inv: bfloat16 [8, 32, 2, 256, 256], P('leaf', 'blk'), as said below
- sub_panels: bfloat16 [8, 32, 2, 256, 256], P('leaf', 'blk')
- sub_parents: int32 [8, 32, 2], P('leaf', 'blk'), may hold values from 0 to 1
Outputs:
- sub_sigma: float32 [8, 32, 2, 256, 256], P('leaf', 'blk')
- top_sigma: float32 [8, 2, 256, 256], P('leaf')
Inputs may be any that keep to these rules, and one draw needn't show every extreme that they name: `root_sigma`: every block is symmetric. `top_inv`: every block is lower triangular with a positive diagonal. `sub_inv`: every block is lower triangular with a positive diagonal.
All inputs are finite; a program needn't handle non-finite values.
Results may differ from a plain program's by a relative error of at most 0.0003.
Values may be sent and summed in bfloat16 or wider, within the bound.
A program may use at most 64 MiB of HBM per device.

v0:
```python
import jax
import jax.numpy as jnp
from jax import lax
from jax.sharding import PartitionSpec as P

HIGH = lax.Precision.HIGHEST


def from_behind(shard, axis, by):
    count = lax.axis_size(axis)
    pairs = [(i, i + by) for i in range(count) if 0 <= i + by < count]
    return lax.ppermute(shard, axis, pairs)


def parent_table(parents, node_count):
    return (parents[:, None] == jnp.arange(node_count, dtype=jnp.int32)[None, :]).astype(
        jnp.float32
    )


def apply_node(inverse, panels, parent_hot, above):
    picked = jnp.einsum("kn,nij->kij", parent_hot, above, precision=HIGH)
    wide_inv = inverse.astype(jnp.float32)
    wide_pan = panels.astype(jnp.float32)
    carried = jnp.einsum("kij,kjm->kim", wide_pan, wide_inv, precision=HIGH)
    own_part = jnp.einsum("kji,kjm->kim", wide_inv, wide_inv, precision=HIGH)
    inner_sum = jnp.einsum("kij,kjm->kim", picked, carried, precision=HIGH)
    return own_part + jnp.einsum("kji,kjm->kim", carried, inner_sum, precision=HIGH)


def on_device(root_sigma, top_inv, top_panels, top_parents, sub_inv, sub_panels, sub_parents):
    node_count = root_sigma.shape[0]
    top_hot = parent_table(top_parents[0], node_count)
    sub_hot = parent_table(sub_parents[0, 0], node_count)
    top_inv_local = top_inv[0]
    top_panel_local = top_panels[0]
    sub_inv_local = sub_inv[0, 0]
    sub_panel_local = sub_panels[0, 0]
    leaf_at = lax.axis_index("leaf")
    blk_at = lax.axis_index("blk")
    leaf_count = lax.axis_size("leaf")
    blk_count = lax.axis_size("blk")
    current = apply_node(top_inv_local, top_panel_local, top_hot, root_sigma)
    for bit_index in range(leaf_count.bit_length() - 1):
        step_size = 1 << bit_index
        incoming = from_behind(current, "leaf", step_size)
        active = (leaf_at >= step_size) & (leaf_at < 2 * step_size)
        current = jnp.where(
            active, apply_node(top_inv_local, top_panel_local, top_hot, incoming), current
        )
    running = apply_node(sub_inv_local, sub_panel_local, sub_hot, current)
    for bit_index in range(blk_count.bit_length() - 1):
        step_size = 1 << bit_index
        incoming = from_behind(running, "blk", step_size)
        active = (blk_at >= step_size) & (blk_at < 2 * step_size)
        running = jnp.where(
            active, apply_node(sub_inv_local, sub_panel_local, sub_hot, incoming), running
        )
    return (running[None, None], current[None])


def solution(mesh):
    in_specs = (
        P(),
        P("leaf", None, None, None),
        P("leaf", None, None, None),
        P("leaf", None),
        P("leaf", "blk", None, None, None),
        P("leaf", "blk", None, None, None),
        P("leaf", "blk", None),
    )
    out_specs = (P("leaf", "blk", None, None, None), P("leaf", None, None, None))
    return jax.shard_map(
        on_device, mesh=mesh, in_specs=in_specs, out_specs=out_specs, check_vma=False
    )
```

profile of v0, /device:TPU:174, one launch (start us, length us, event | category | flops | bytes accessed | tf_op | source)
XLA Modules:
  0.0 173.3 jit_solution(8234889099940066060)
XLA Ops:
  0.7 1.4 fusion.52
  3.0 1.3 fusion.47
  4.3 0.7 fusion.27
  4.9 1.0 convolution_add_fusion.9
  6.0 2.9 %collective-permute-start = (f32[2,256,256]{2,1,0:T(8,128)S(1)}, f32[2,256,256]{2,1,0:T(8,128)S(1)}, u32[]{:S(2)}, u32[]{:S(2)}) collective-permute-start(f32[2,256,256]{2,1,0:T(8,128)S(1)} %convolution_add_fusion.9), channel_id=1, source_target_pairs={{0,32},{32,64},{64,96},{96,128},{128,160},{160,192},{192,224},{1,3... | collective-permute-start | bytes 1572872 | tf_op jit(solution)/shard_map/ppermute | solution.py:12
  8.9 12.6 %collective-permute-done = f32[2,256,256]{2,1,0:T(8,128)S(1)} collective-permute-done((f32[2,256,256]{2,1,0:T(8,128)S(1)}, f32[2,256,256]{2,1,0:T(8,128)S(1)}, u32[]{:S(2)}, u32[]{:S(2)}) %collective-permute-start) | collective-permute-done | bytes 524320 | tf_op jit(solution)/shard_map/ppermute | solution.py:12
  21.5 1.3 fusion.45
  22.9 0.7 fusion.25
  23.5 1.0 fusion.8
  24.6 3.4 %collective-permute-start.1 = (f32[2,256,256]{2,1,0:T(8,128)S(1)}, f32[2,256,256]{2,1,0:T(8,128)S(1)}, u32[]{:S(2)}, u32[]{:S(2)}) collective-permute-start(f32[2,256,256]{2,1,0:T(8,128)S(1)} %fusion.8), channel_id=1, source_target_pairs={{0,64},{32,96},{64,128},{96,160},{128,192},{160,224},{1,65},{33,97... | collective-permute-start | bytes 1572872 | tf_op jit(solution)/shard_map/ppermute | solution.py:12
  28.0 21.6 %collective-permute-done.1 = f32[2,256,256]{2,1,0:T(8,128)S(1)} collective-permute-done((f32[2,256,256]{2,1,0:T(8,128)S(1)}, f32[2,256,256]{2,1,0:T(8,128)S(1)}, u32[]{:S(2)}, u32[]{:S(2)}) %collective-permute-start.1) | collective-permute-done | bytes 524320 | tf_op jit(solution)/shard_map/ppermute | solution.py:12
  49.6 1.3 fusion.43
  50.9 0.7 fusion.23
  51.9 1.0 fusion.7
  53.0 1.5 collective-permute-start.2
  54.8 0.7 copy-done.9
  55.7 26.5 %collective-permute-done.2 = f32[2,256,256]{2,1,0:T(8,128)} collective-permute-done((f32[2,256,256]{2,1,0:T(8,128)S(1)}, f32[2,256,256]{2,1,0:T(8,128)}, u32[]{:S(2)}, u32[]{:S(2)}) %collective-permute-start.2) | collective-permute-done | bytes 524320 | tf_op jit(solution)/shard_map/ppermute | solution.py:12
  82.2 2.4 %fusion.41 = f32[2,256,256]{2,0,1:T(2,128)S(1)} fusion(f32[2,256,256]{2,1,0:T(8,128)} %collective-permute-done.2, s32[2]{0:T(128)S(1)} %bitcast.83), kind=kOutput, calls=%fused_computation.51 | convolution fusion | flops 3145732 | bytes 1048584 | tf_op jit(solution)/shard_map/kn,nij->kij/dot_general | solution.py:22
  84.6 0.7 fusion.21
  85.6 1.0 fusion.6
  86.7 0.7 copy-done.10
  87.3 1.3 fusion.39
  88.7 0.7 fusion.19
  89.3 1.0 convolution_add_fusion.5
  90.4 1.9 %collective-permute-start.3 = (f32[2,256,256]{2,1,0:T(8,128)S(1)}, f32[2,256,256]{2,1,0:T(8,128)S(1)}, u32[]{:S(2)}, u32[]{:S(2)}) collective-permute-start(f32[2,256,256]{2,1,0:T(8,128)S(1)} %convolution_add_fusion.5), channel_id=1, source_target_pairs={{0,1},{1,2},{2,3},{3,4},{4,5},{5,6},{6,7},{7,8},{8,9},{9,10},{10,1... | collective-permute-start | bytes 1572872 | tf_op jit(solution)/shard_map/ppermute | solution.py:12
  92.3 8.6 %collective-permute-done.3 = f32[2,256,256]{2,1,0:T(8,128)S(1)} collective-permute-done((f32[2,256,256]{2,1,0:T(8,128)S(1)}, f32[2,256,256]{2,1,0:T(8,128)S(1)}, u32[]{:S(2)}, u32[]{:S(2)}) %collective-permute-start.3) | collective-permute-done | bytes 524320 | tf_op jit(solution)/shard_map/ppermute | solution.py:12
  100.9 1.3 fusion.37
  102.8 1.1 fusion.5
  103.9 3.7 %collective-permute-start.4 = (f32[2,256,256]{2,1,0:T(8,128)S(1)}, f32[2,256,256]{2,1,0:T(8,128)S(1)}, u32[]{:S(2)}, u32[]{:S(2)}) collective-permute-start(f32[2,256,256]{2,1,0:T(8,128)S(1)} %fusion.5), channel_id=1, source_target_pairs={{0,2},{1,3},{2,4},{3,5},{4,6},{5,7},{6,8},{7,9},{8,10},{9,11},{10,... | collective-permute-start | bytes 1572872 | tf_op jit(solution)/shard_map/ppermute | solution.py:12
  107.6 11.2 %collective-permute-done.4 = f32[2,256,256]{2,1,0:T(8,128)S(1)} collective-permute-done((f32[2,256,256]{2,1,0:T(8,128)S(1)}, f32[2,256,256]{2,1,0:T(8,128)S(1)}, u32[]{:S(2)}, u32[]{:S(2)}) %collective-permute-start.4) | collective-permute-done | bytes 524320 | tf_op jit(solution)/shard_map/ppermute | solution.py:12
  118.8 1.3 fusion.35
  120.1 0.7 fusion.15
  120.8 1.0 fusion.4
  121.9 2.9 %collective-permute-start.5 = (f32[2,256,256]{2,1,0:T(8,128)S(1)}, f32[2,256,256]{2,1,0:T(8,128)S(1)}, u32[]{:S(2)}, u32[]{:S(2)}) collective-permute-start(f32[2,256,256]{2,1,0:T(8,128)S(1)} %fusion.4), channel_id=1, source_target_pairs={{0,4},{1,5},{2,6},{3,7},{4,8},{5,9},{6,10},{7,11},{8,12},{9,13},{1... | collective-permute-start | bytes 1572872 | tf_op jit(solution)/shard_map/ppermute | solution.py:12
  124.8 12.9 %collective-permute-done.5 = f32[2,256,256]{2,1,0:T(8,128)S(1)} collective-permute-done((f32[2,256,256]{2,1,0:T(8,128)S(1)}, f32[2,256,256]{2,1,0:T(8,128)S(1)}, u32[]{:S(2)}, u32[]{:S(2)}) %collective-permute-start.5) | collective-permute-done | bytes 524320 | tf_op jit(solution)/shard_map/ppermute | solution.py:12
  137.7 1.3 fusion.33
  139.1 0.7 fusion.13
  139.7 1.1 fusion.3
  140.8 1.3 collective-permute-start.6
  142.1 11.2 %collective-permute-done.6 = f32[2,256,256]{2,1,0:T(8,128)S(1)} collective-permute-done((f32[2,256,256]{2,1,0:T(8,128)S(1)}, f32[2,256,256]{2,1,0:T(8,128)S(1)}, u32[]{:S(2)}, u32[]{:S(2)}) %collective-permute-start.6) | collective-permute-done | bytes 524320 | tf_op jit(solution)/shard_map/ppermute | solution.py:12
  153.3 1.3 fusion.31
  154.6 0.7 fusion.11
  155.3 1.0 fusion.2
  156.4 1.6 collective-permute-start.7
  157.9 11.6 %collective-permute-done.7 = f32[2,256,256]{2,1,0:T(8,128)S(1)} collective-permute-done((f32[2,256,256]{2,1,0:T(8,128)S(1)}, f32[2,256,256]{2,1,0:T(8,128)S(1)}, u32[]{:S(2)}, u32[]{:S(2)}) %collective-permute-start.7) | collective-permute-done | bytes 524320 | tf_op jit(solution)/shard_map/ppermute | solution.py:12
  169.5 1.3 fusion.29
  170.8 0.7 fusion.9
  171.5 1.8 %fusion.1 = f32[1,1,2,256,256]{4,3,2,1,0:T(8,128)} fusion(f32[2,256,256]{2,1,0:T(8,128)S(1)} %fusion.2, f32[2,256,256]{2,1,0:T(8,128)S(1)} %fusion.57, f32[2,256,256]{2,1,0:T(8,128)S(1)} %fusion.54, f32[2,256,256]{2,1,0:T(8,128)S(1)} %fusion.9, pred[]{:T(512)S(6)} %and.26), kind=kOutput, calls=%fused_computation.2 | convolution fusion | flops 402915328 | bytes 2621441 | tf_op jit(solution)/shard_map/kji,kjm->kim/dot_general | solution.py:28
  (26 shorter events, 2.8 us)
Async XLA Ops:
  0.6 1.7 copy-start
  0.6 1.4 copy-start.6
  0.7 1.4 copy-start.8
  2.3 0.7 copy-start.11
  6.0 15.6 %collective-permute-start = (f32[2,256,256]{2,1,0:T(8,128)S(1)}, f32[2,256,256]{2,1,0:T(8,128)S(1)}, u32[]{:S(2)}, u32[]{:S(2)}) collective-permute-start(f32[2,256,256]{2,1,0:T(8,128)S(1)} %convolution_add_fusion.9), channel_id=1, source_target_pairs={{0,32},{32,64},{64,96},{96,128},{128,160},{160,192},{192,224},{1,3... | collective-permute-start | bytes 1572872 | tf_op jit(solution)/shard_map/ppermute | solution.py:12
  24.6 3.4 %copy-start.4 = (f32[2,256,256]{2,1,0:T(8,128)}, f32[2,256,256]{2,1,0:T(8,128)S(1)}, u32[]{:S(2)}) copy-start(f32[2,256,256]{2,1,0:T(8,128)S(1)} %fusion.8) | copy-start | bytes 1572868
  24.6 25.0 %collective-permute-start.1 = (f32[2,256,256]{2,1,0:T(8,128)S(1)}, f32[2,256,256]{2,1,0:T(8,128)S(1)}, u32[]{:S(2)}, u32[]{:S(2)}) collective-permute-start(f32[2,256,256]{2,1,0:T(8,128)S(1)} %fusion.8), channel_id=1, source_target_pairs={{0,64},{32,96},{64,128},{96,160},{128,192},{160,224},{1,65},{33,97... | collective-permute-start | bytes 1572872 | tf_op jit(solution)/shard_map/ppermute | solution.py:12
  50.9 1.0 copy-start.5
  51.9 2.6 %copy-start.7 = (bf16[1,1,2,256,256]{4,3,2,1,0:T(8,128)(2,1)S(1)}, bf16[1,1,2,256,256]{4,3,2,1,0:T(8,128)(2,1)}, u32[]{:S(2)}) copy-start(bf16[1,1,2,256,256]{4,3,2,1,0:T(8,128)(2,1)} %param.11) | copy-start | bytes 786436
  53.0 2.7 %copy-start.2 = (f32[2,256,256]{2,1,0:T(8,128)}, f32[2,256,256]{2,1,0:T(8,128)S(1)}, u32[]{:S(2)}) copy-start(f32[2,256,256]{2,1,0:T(8,128)S(1)} %fusion.7) | copy-start | bytes 1572868
  53.0 29.2 %collective-permute-start.2 = (f32[2,256,256]{2,1,0:T(8,128)S(1)}, f32[2,256,256]{2,1,0:T(8,128)}, u32[]{:S(2)}, u32[]{:S(2)}) collective-permute-start(f32[2,256,256]{2,1,0:T(8,128)S(1)} %fusion.7), channel_id=1, source_target_pairs={{0,128},{32,160},{64,192},{96,224},{1,129},{33,161},{65,193},{97,2... | collective-permute-start | bytes 1572872 | tf_op jit(solution)/shard_map/ppermute | solution.py:12
  54.5 1.0 copy-start.9
  84.6 1.0 copy-start.3
  86.7 2.0 %copy-start.1 = (f32[2,256,256]{2,1,0:T(8,128)}, f32[2,256,256]{2,1,0:T(8,128)S(1)}, u32[]{:S(2)}) copy-start(f32[2,256,256]{2,1,0:T(8,128)S(1)} %fusion.6) | copy-start | bytes 1572868
  86.7 0.7 copy-start.10
  90.4 10.5 %collective-permute-start.3 = (f32[2,256,256]{2,1,0:T(8,128)S(1)}, f32[2,256,256]{2,1,0:T(8,128)S(1)}, u32[]{:S(2)}, u32[]{:S(2)}) collective-permute-start(f32[2,256,256]{2,1,0:T(8,128)S(1)} %convolution_add_fusion.5), channel_id=1, source_target_pairs={{0,1},{1,2},{2,3},{3,4},{4,5},{5,6},{6,7},{7,8},{8,9},{9,10},{10,1... | collective-permute-start | bytes 1572872 | tf_op jit(solution)/shard_map/ppermute | solution.py:12
  103.9 14.9 %collective-permute-start.4 = (f32[2,256,256]{2,1,0:T(8,128)S(1)}, f32[2,256,256]{2,1,0:T(8,128)S(1)}, u32[]{:S(2)}, u32[]{:S(2)}) collective-permute-start(f32[2,256,256]{2,1,0:T(8,128)S(1)} %fusion.5), channel_id=1, source_target_pairs={{0,2},{1,3},{2,4},{3,5},{4,6},{5,7},{6,8},{7,9},{8,10},{9,11},{10,... | collective-permute-start | bytes 1572872 | tf_op jit(solution)/shard_map/ppermute | solution.py:12
  121.9 15.9 %collective-permute-start.5 = (f32[2,256,256]{2,1,0:T(8,128)S(1)}, f32[2,256,256]{2,1,0:T(8,128)S(1)}, u32[]{:S(2)}, u32[]{:S(2)}) collective-permute-start(f32[2,256,256]{2,1,0:T(8,128)S(1)} %fusion.4), channel_id=1, source_target_pairs={{0,4},{1,5},{2,6},{3,7},{4,8},{5,9},{6,10},{7,11},{8,12},{9,13},{1... | collective-permute-start | bytes 1572872 | tf_op jit(solution)/shard_map/ppermute | solution.py:12
  140.8 12.6 %collective-permute-start.6 = (f32[2,256,256]{2,1,0:T(8,128)S(1)}, f32[2,256,256]{2,1,0:T(8,128)S(1)}, u32[]{:S(2)}, u32[]{:S(2)}) collective-permute-start(f32[2,256,256]{2,1,0:T(8,128)S(1)} %fusion.3), channel_id=1, source_target_pairs={{0,8},{1,9},{2,10},{3,11},{4,12},{5,13},{6,14},{7,15},{8,16},{9,17... | collective-permute-start | bytes 1572872 | tf_op jit(solution)/shard_map/ppermute | solution.py:12
  156.4 13.1 %collective-permute-start.7 = (f32[2,256,256]{2,1,0:T(8,128)S(1)}, f32[2,256,256]{2,1,0:T(8,128)S(1)}, u32[]{:S(2)}, u32[]{:S(2)}) collective-permute-start(f32[2,256,256]{2,1,0:T(8,128)S(1)} %fusion.2), channel_id=1, source_target_pairs={{0,16},{1,17},{2,18},{3,19},{4,20},{5,21},{6,22},{7,23},{8,24},{9,... | collective-permute-start | bytes 1572872 | tf_op jit(solution)/shard_map/ppermute | solution.py:12
where the time goes:
time: 174 us; the launch traced here: 173 us
  waiting for transfers between devices  116 us (67%)
  matrix products  34 us (20%)
  starting transfers between devices  19.2 us (11%)
  local copies, waits for them, and re-layouts  2.78 us (2%)
    ppermute x8, waiting for transfers between devices, from_behind(): return lax.ppermute(shard, axis, pairs)  116 us
    ppermute x8, starting transfers between devices, from_behind(): return lax.ppermute(shard, axis, pairs)  19.2 us
    dot_general x10, matrix products, apply_node(): picked = jnp.einsum('kn,nij->kij', parent_hot, above, precision=HIGH)  14.1 us
    dot_general x10, matrix products, apply_node(): jnp.einsum('kji,kjm->kim', carried, inner_sum, precision=HIGH)  11.3 us
    dot_general x10, matrix products, apply_node(): inner_sum = jnp.einsum('kij,kjm->kim', picked, carried, precision=HIGH)  6.52 us
  transfers between devices with their start and end apart: 8, of which 8 were waited for; matrix products, arithmetic and copies ran while one was open for 0% of the time, Pallas kernels for 0%

commit v1 on v0

v1 whole, which is shorter than its diff:
```python
import functools

import jax
import jax.numpy as jnp
from jax import lax
from jax.experimental import pallas as pl
from jax.experimental.pallas import tpu as pltpu
from jax.sharding import PartitionSpec as P

MESH = pl.DeviceIdType.MESH
F32 = jnp.float32
BF16 = jnp.bfloat16
B = 256
H = 128
ROWS = 896
CH = 8
CROWS = ROWS // CH
ZCH = CH // 2

T0, T1, T2, T3, TOWN, RX, R1, OWN, Y0, Y1, D0 = range(11)
NSLOT = 11
(S_T0P, S_T0M, S_T1, S_T2, S_T3, S_D0, S_D1, S_D2, S_D3,
 S_XA, S_XB, S_R1, S_YA, S_YB, S_Y1, S_DD) = range(16)
NSEND = 16


def split(value):
    high = value.astype(BF16)
    return high, (value - high.astype(F32)).astype(BF16)


def pick(options, index):
    result = jnp.int32(options[0])
    for at in range(1, len(options)):
        result = jnp.where(index == at, jnp.int32(options[at]), result)
    return result


def kernel(root_ref, tinv_ref, tpan_ref, tpar_ref, sinv_ref, span_ref, spar_ref,
           sub_ref, top_ref, slots, x_ref, send_sem, recv_sem):
    z = lax.axis_index("leaf")
    blk = lax.axis_index("blk")
    x = blk // 8
    y = (blk // 2) % 4
    c = blk % 2

    def dev(zz, xx, yy, cc):
        return (zz, xx * 8 + yy * 2 + cc)

    zp, zm = dev((z + 1) % 8, x, y, c), dev((z + 7) % 8, x, y, c)
    xp, xm = dev(z, (x + 1) % 4, y, c), dev(z, (x + 3) % 4, y, c)
    yp, ym = dev(z, x, (y + 1) % 4, c), dev(z, x, (y + 3) % 4, c)
    other = dev(z, x, y, 1 - c)

    barrier = pltpu.get_barrier_semaphore()
    for where in (zp, zm, xp, xm, yp, ym, other):
        pl.semaphore_signal(barrier, inc=1, device_id=where, device_id_type=MESH)

    rows_at = lax.broadcasted_iota(jnp.int32, (H, H), 0)
    cols_at = lax.broadcasted_iota(jnp.int32, (H, H), 1)
    corner = (rows_at == 0) & (cols_at == H - 1)

    def pack(inv, pan, par, slot):
        slots[slot, 0:B, :] = pan(0)
        slots[slot, B:2 * B, :] = pan(1)
        for k in range(2):
            v = inv(k)
            slots[slot, 2 * B + k * H:2 * B + (k + 1) * H, :] = v[H:, :]
            quarter = jnp.where(corner, par(k).astype(F32), v[:H, :H].astype(F32))
            slots[slot, 3 * B:3 * B + H, k * H:(k + 1) * H] = quarter.astype(BF16)

    pack(lambda k: tinv_ref[0, k], lambda k: tpan_ref[0, k], lambda k: tpar_ref[0, k],
         jnp.minimum(z, 4))
    pack(lambda k: sinv_ref[0, 0, k], lambda k: span_ref[0, 0, k], lambda k: spar_ref[0, 0, k],
         RX + jnp.minimum(x, 2))
    x_ref[...] = root_ref[...]

    pl.semaphore_wait(barrier, 7)

    def copy(src, dst, k, sid, where):
        rows = pl.ds(pl.multiple_of(k * CROWS, CROWS), CROWS)
        return pltpu.make_async_remote_copy(
            src_ref=slots.at[src, rows, :], dst_ref=slots.at[dst, rows, :],
            send_sem=send_sem.at[sid, k], recv_sem=recv_sem.at[dst, k],
            device_id=where, device_id_type=MESH)

    def arrived(slot, k):
        copy(slot, slot, k, 0, other).wait_recv()

    zflows = (
        (T0, jnp.where(z < 4, z, 8 - z), z >= 0, z >= 1,
         ((S_T0P, zp, z < 3), (S_T0M, zm, (z == 0) | (z > 4)))),
        (T1, z - 1, z >= 1, (z == 3) | (z == 5) | (z == 7), ((S_T1, zp, z < 7),)),
        (T2, (10 - z) % 8, (10 - z) % 8 <= 4, z == 6, ((S_T2, zm, z != 6),)),
        (T3, z - 3, z >= 3, z == 7, ((S_T3, zp, z < 7),)),
    )
    rx_depth = pick((0, 1, 2, 1), x)
    y0_depth = rx_depth + pick((0, 1, 2, 1), y)
    y1_depth = rx_depth + y - 1

    pflows = (
        (RX, rx_depth, x >= 0, (
            (RX, S_XA, xp, x == 0), (RX, S_XB, xm, (x == 0) | (x == 3)),
            (Y0, S_YA, yp, y == 0), (Y0, S_YB, ym, y == 0),
            (Y1, S_Y1, yp, y == 1), (D0, S_DD, other, (c == 0) & (y == 0)))),
        (R1, x - 1, x >= 1, ((R1, S_R1, xp, x < 3),)),
        (Y0, y0_depth, y >= 1, (
            (Y0, S_YB, ym, y == 3), (D0, S_DD, other, c == 0))),
        (Y1, y1_depth, y >= 2, ((Y1, S_Y1, yp, y == 2),)),
        (D0, jnp.where(y == 0, rx_depth, y0_depth) + 1, c == 1, ()),
    )

    def relay(t, carry):
        for at, (slot, depth, member, needed, outs) in enumerate(zflows):
            j = t - depth

            @pl.when(member & (j >= 0) & (j < ZCH))
            def _():
                k = c * ZCH + j

                @pl.when(depth > 0)
                def _():
                    arrived(slot, k)

                for sid, where, when in outs:
                    @pl.when(when)
                    def _():
                        copy(slot, slot, k, sid, where).start()

                @pl.when(needed & (depth > 0))
                def _():
                    copy(slot, slot, k, S_D0 + at, other).start()

        for slot, depth, member, outs in pflows:
            k = t - depth

            @pl.when(member & (k >= 0) & (k < CH))
            def _():
                @pl.when(depth > 0)
                def _():
                    arrived(slot, k)

                for dst, sid, where, when in outs:
                    @pl.when(when)
                    def _():
                        copy(slot, dst, k, sid, where).start()
        return carry

    lax.fori_loop(0, CH + 5, relay, 0)

    def late(j, carry):
        for slot, depth, member, needed, outs in zflows:
            @pl.when(needed & (depth > 0))
            def _():
                arrived(slot, (1 - c) * ZCH + j)
        return carry

    lax.fori_loop(0, ZCH, late, 0)

    tri = rows_at >= cols_at

    def step(s, carry):
        slot = pick((T0, T1, jnp.int32(2) + z % 2, TOWN, D0, jnp.where(y == 0, RX, Y0), Y1, RX, R1,
                     jnp.where(x == 1, R1, OWN)), s)
        active = pick((1, z % 2, (z // 2) % 2, z // 4, c, 1, (y == 3).astype(jnp.int32),
                       (y >= 1).astype(jnp.int32), (x == 3).astype(jnp.int32),
                       (x >= 1).astype(jnp.int32)), s)

        @pl.when(active == 1)
        def _():
            above0, above1 = x_ref[0], x_ref[1]
            for k in range(2):
                panel = slots[slot, k * B:(k + 1) * B, :]
                low = slots[slot, 2 * B + k * H:2 * B + (k + 1) * H, :]
                quarter = slots[slot, 3 * B:3 * B + H, k * H:(k + 1) * H].astype(F32)
                second = quarter[0:1, H - 1:H] > 0.5
                quarter = jnp.where(tri, quarter, 0.0).astype(BF16)
                v = jnp.concatenate(
                    [jnp.concatenate([quarter, jnp.zeros((H, H), BF16)], axis=1), low], axis=0)
                own = lax.dot_general(v, v, (((0,), (0,)), ((), ())), preferred_element_type=F32)
                carried = jnp.dot(panel, v, preferred_element_type=F32)
                ch, cl = split(carried)
                th, tl = split(carried.T)
                xh, xl = split(jnp.where(second, above1, above0))
                u = jnp.dot(jnp.concatenate([th, tl, th], axis=1),
                            jnp.concatenate([xh, xh, xl], axis=0), preferred_element_type=F32)
                uh, ul = split(u)
                x_ref[k] = own + jnp.dot(
                    jnp.concatenate([uh, ul, uh], axis=1),
                    jnp.concatenate([ch, ch, cl], axis=0), preferred_element_type=F32)

        @pl.when(s == 3)
        def _():
            top_ref[0] = x_ref[...]
        return carry

    lax.fori_loop(0, 10, step, 0)
    sub_ref[0, 0] = x_ref[...]

    def drain_z(j, carry):
        for at, (slot, depth, member, needed, outs) in enumerate(zflows):
            @pl.when(member)
            def _():
                k = c * ZCH + j
                for sid, where, when in outs:
                    @pl.when(when)
                    def _():
                        copy(slot, slot, k, sid, where).wait_send()

                @pl.when(needed & (depth > 0))
                def _():
                    copy(slot, slot, k, S_D0 + at, other).wait_send()
        return carry

    def drain_p(k, carry):
        for slot, depth, member, outs in pflows:
            @pl.when(member)
            def _():
                for dst, sid, where, when in outs:
                    @pl.when(when)
                    def _():
                        copy(slot, dst, k, sid, where).wait_send()
        return carry

    lax.fori_loop(0, ZCH, drain_z, 0)
    lax.fori_loop(0, CH, drain_p, 0)


def on_device(root_sigma, top_inv, top_panels, top_parents, sub_inv, sub_panels, sub_parents):
    vmem = pl.BlockSpec(memory_space=pltpu.VMEM)
    smem = pl.BlockSpec(memory_space=pltpu.SMEM)
    return pl.pallas_call(
        kernel,
        out_shape=(jax.ShapeDtypeStruct((1, 1, 2, B, B), F32),
                   jax.ShapeDtypeStruct((1, 2, B, B), F32)),
        in_specs=[vmem, vmem, vmem, smem, vmem, vmem, smem],
        out_specs=(vmem, vmem),
        scratch_shapes=[
            pltpu.VMEM((NSLOT, ROWS, B), BF16),
            pltpu.VMEM((2, B, B), F32),
            pltpu.SemaphoreType.DMA((NSEND, CH)),
            pltpu.SemaphoreType.DMA((NSLOT, CH)),
        ],
        compiler_params=pltpu.CompilerParams(
            collective_id=0, has_side_effects=True, vmem_limit_bytes=40 << 20),
    )(root_sigma, top_inv, top_panels, top_parents, sub_inv, sub_panels, sub_parents)


def solution(mesh):
    in_specs = (
        P(),
        P("leaf", None, None, None),
        P("leaf", None, None, None),
        P("leaf", None),
        P("leaf", "blk", None, None, None),
        P("leaf", "blk", None, None, None),
        P("leaf", "blk", None),
    )
    out_specs = (P("leaf", "blk", None, None, None), P("leaf", None, None, None))
    return jax.shard_map(
        on_device, mesh=mesh, in_specs=in_specs, out_specs=out_specs, check_vma=False
    )
```

time: 174 us -> 63.7 us (0.37)
  the two profiles are of different devices: /device:TPU:174 before, /device:TPU:245 now
where the time goes in v1:
time: 63.7 us; the launch traced here: 63.4 us
  Pallas kernels  55 us (86%)
  local copies, waits for them, and re-layouts  7.73 us (12%)
  between operations  0.66 us (1%)
    pallas_call x1, Pallas kernels, on_device(): pl.pallas_call(kernel, out_shape=(jax.ShapeDtypeStruct((1, 1, 2, B, B), F...  55 us
    unnamed x16, local copies, waits for them, and re-layouts  7.73 us

profile of v1, /device:TPU:245, one launch (start us, length us, event | category | flops | bytes accessed | tf_op | source)
XLA Modules:
  0.0 63.4 jit_solution(9817709305961730925)
XLA Ops:
  0.6 0.0 copy-start
  0.6 1.0 %copy-done = f32[2,256,256]{2,1,0:T(8,128)S(1)} copy-done((f32[2,256,256]{2,1,0:T(8,128)S(1)}, f32[2,256,256]{2,1,0:T(8,128)}, u32[]{:S(2)}) %copy-start) | copy-done | bytes 524312
  1.7 0.0 copy-start.1
  1.7 0.9 %copy-done.1 = bf16[1,2,256,256]{3,2,1,0:T(8,128)(2,1)S(1)} copy-done((bf16[1,2,256,256]{3,2,1,0:T(8,128)(2,1)S(1)}, bf16[1,2,256,256]{3,2,1,0:T(8,128)(2,1)}, u32[]{:S(2)}) %copy-start.1) | copy-done | bytes 262168
  2.6 0.0 copy-start.2
  2.6 0.9 %copy-done.2 = bf16[1,2,256,256]{3,2,1,0:T(8,128)(2,1)S(1)} copy-done((bf16[1,2,256,256]{3,2,1,0:T(8,128)(2,1)S(1)}, bf16[1,2,256,256]{3,2,1,0:T(8,128)(2,1)}, u32[]{:S(2)}) %copy-start.2) | copy-done | bytes 262168
  3.6 0.0 copy-start.3
  3.6 0.9 %copy-done.3 = bf16[1,1,2,256,256]{4,3,2,1,0:T(8,128)(2,1)S(1)} copy-done((bf16[1,1,2,256,256]{4,3,2,1,0:T(8,128)(2,1)S(1)}, bf16[1,1,2,256,256]{4,3,2,1,0:T(8,128)(2,1)}, u32[]{:S(2)}) %copy-start.3) | copy-done | bytes 262168
  4.5 0.0 copy-start.4
  4.5 0.9 %copy-done.4 = bf16[1,1,2,256,256]{4,3,2,1,0:T(8,128)(2,1)S(1)} copy-done((bf16[1,1,2,256,256]{4,3,2,1,0:T(8,128)(2,1)S(1)}, bf16[1,1,2,256,256]{4,3,2,1,0:T(8,128)(2,1)}, u32[]{:S(2)}) %copy-start.4) | copy-done | bytes 262168
  5.5 0.0 copy-start.5
  5.5 0.7 %copy-done.5 = s32[1,2]{1,0:T(1,128)S(1)} copy-done((s32[1,2]{1,0:T(1,128)S(1)}, s32[1,2]{1,0:T(1,128)}, u32[]{:S(2)}) %copy-start.5) | copy-done | bytes 32
  6.1 0.0 copy-start.6
  6.1 0.7 %copy-done.6 = s32[1,1,2]{2,1,0:T(1,128)S(1)} copy-done((s32[1,1,2]{2,1,0:T(1,128)S(1)}, s32[1,1,2]{2,1,0:T(1,128)}, u32[]{:S(2)}) %copy-start.6) | copy-done | bytes 32
  6.8 55.0 %shard_map.86 = (f32[1,1,2,256,256]{4,3,2,1,0:T(8,128)S(1)}, f32[1,2,256,256]{3,2,1,0:T(8,128)S(1)}) custom-call(f32[2,256,256]{2,1,0:T(8,128)S(1)} %copy-done, bf16[1,2,256,256]{3,2,1,0:T(8,128)(2,1)S(1)} %copy-done.1, bf16[1,2,256,256]{3,2,1,0:T(8,128)(2,1)S(1)} %copy-done.2, s32[1,2]{1,0:T(1,128)S(1)} %copy-done.5, ...), custom_call_target="tpu_custom_call" | custom-call | tf_op jit(solution)/shard_map/pallas_call | solution.py:232
  61.8 0.8 %copy.11 = f32[1,1,2,256,256]{4,3,2,1,0:T(8,128)} copy(f32[1,1,2,256,256]{4,3,2,1,0:T(8,128)S(1)} %get-tuple-element.4) | data formatting | bytes 1048576
  62.6 0.8 %copy.12 = f32[1,2,256,256]{3,2,1,0:T(8,128)} copy(f32[1,2,256,256]{3,2,1,0:T(8,128)S(1)} %get-tuple-element.5) | data formatting | bytes 1048576
Async XLA Ops:
  0.6 1.0 %copy-start = (f32[2,256,256]{2,1,0:T(8,128)S(1)}, f32[2,256,256]{2,1,0:T(8,128)}, u32[]{:S(2)}) copy-start(f32[2,256,256]{2,1,0:T(8,128)} %root_ref.1) | copy-start | bytes 1572868
  1.7 0.9 %copy-start.1 = (bf16[1,2,256,256]{3,2,1,0:T(8,128)(2,1)S(1)}, bf16[1,2,256,256]{3,2,1,0:T(8,128)(2,1)}, u32[]{:S(2)}) copy-start(bf16[1,2,256,256]{3,2,1,0:T(8,128)(2,1)} %tinv_ref.1) | copy-start | bytes 786436
  2.6 0.9 %copy-start.2 = (bf16[1,2,256,256]{3,2,1,0:T(8,128)(2,1)S(1)}, bf16[1,2,256,256]{3,2,1,0:T(8,128)(2,1)}, u32[]{:S(2)}) copy-start(bf16[1,2,256,256]{3,2,1,0:T(8,128)(2,1)} %tpan_ref.1) | copy-start | bytes 786436
  3.6 0.9 %copy-start.3 = (bf16[1,1,2,256,256]{4,3,2,1,0:T(8,128)(2,1)S(1)}, bf16[1,1,2,256,256]{4,3,2,1,0:T(8,128)(2,1)}, u32[]{:S(2)}) copy-start(bf16[1,1,2,256,256]{4,3,2,1,0:T(8,128)(2,1)} %sinv_ref.1) | copy-start | bytes 786436
  4.5 0.9 %copy-start.4 = (bf16[1,1,2,256,256]{4,3,2,1,0:T(8,128)(2,1)S(1)}, bf16[1,1,2,256,256]{4,3,2,1,0:T(8,128)(2,1)}, u32[]{:S(2)}) copy-start(bf16[1,1,2,256,256]{4,3,2,1,0:T(8,128)(2,1)} %span_ref.1) | copy-start | bytes 786436
  5.5 0.7 %copy-start.5 = (s32[1,2]{1,0:T(1,128)S(1)}, s32[1,2]{1,0:T(1,128)}, u32[]{:S(2)}) copy-start(s32[1,2]{1,0:T(1,128)} %tpar_ref.1) | copy-start | bytes 28
  6.1 0.7 %copy-start.6 = (s32[1,1,2]{2,1,0:T(1,128)S(1)}, s32[1,1,2]{2,1,0:T(1,128)}, u32[]{:S(2)}) copy-start(s32[1,1,2]{2,1,0:T(1,128)} %spar_ref.1) | copy-start | bytes 28

commit v2 on v1

v2 whole, which is shorter than its diff:
```python
import functools

import jax
import jax.numpy as jnp
from jax import lax
from jax.experimental import pallas as pl
from jax.experimental.pallas import tpu as pltpu
from jax.sharding import PartitionSpec as P

MESH = pl.DeviceIdType.MESH
F32 = jnp.float32
BF16 = jnp.bfloat16
B = 256
H = 128
ROWS = 896
CH = 7
ZCH = 2
PACE = 2
ZHOP, ZSTEP = 2, 1
ZUP = ZCH // 2
LAST = max(CH + 5, 4 * ZHOP + ZSTEP * ZCH)

T0, T1, T2, T3, TOWN, RX, R1, OWN, Y0, Y1, D0 = range(11)
NSLOT = 11
(S_T0P, S_T0M, S_T1, S_T2, S_T3, S_D0, S_D1, S_D2, S_D3,
 S_XA, S_XB, S_R1, S_YA, S_YB, S_Y1, S_DD, S_T1M, S_T2M) = range(18)
NSEND = 18


def split(value):
    high = value.astype(BF16)
    return high, (value - high.astype(F32)).astype(BF16)


def pick(options, index):
    result = jnp.int32(options[0])
    for at in range(1, len(options)):
        result = jnp.where(index == at, jnp.int32(options[at]), result)
    return result


def kernel(root_ref, tinv_ref, tpan_ref, tpar_ref, sinv_ref, span_ref, spar_ref,
           sub_ref, top_ref, slots, x_ref, own_ref, left_ref, right_ref,
           corners, tpar, spar, local_sem, send_sem, recv_sem):
    z = lax.axis_index("leaf")
    blk = lax.axis_index("blk")
    x = blk // 8
    y = (blk // 2) % 4
    c = blk % 2

    def dev(zz, xx, yy, cc):
        return (zz, xx * 8 + yy * 2 + cc)

    zp, zm = dev((z + 1) % 8, x, y, c), dev((z + 7) % 8, x, y, c)
    xp, xm = dev(z, (x + 1) % 4, y, c), dev(z, (x + 3) % 4, y, c)
    yp, ym = dev(z, x, (y + 1) % 4, c), dev(z, x, (y + 3) % 4, c)
    other = dev(z, x, y, 1 - c)

    barrier = pltpu.get_barrier_semaphore()
    for where in (zp, zm, xp, xm, yp, ym, other):
        pl.semaphore_signal(barrier, inc=1, device_id=where, device_id_type=MESH)

    top_slot = jnp.minimum(z, 4)
    sub_slot = RX + jnp.minimum(x, 2)
    loads = []

    def load(src, dst):
        loads.append(pltpu.make_async_copy(src, dst, local_sem.at[len(loads)]))
        loads[-1].start()

    load(tpar_ref, tpar)
    load(spar_ref, spar)
    for at, slot, inv, pan in ((0, top_slot, tinv_ref.at[0], tpan_ref.at[0]),
                               (1, sub_slot, sinv_ref.at[0, 0], span_ref.at[0, 0])):
        for k in range(2):
            load(inv.at[k, 0:H, 0:H], corners.at[at, k])
            load(pan.at[k], slots.at[slot, k * B:(k + 1) * B, :])
            load(inv.at[k, H:B, :], slots.at[slot, 2 * B + k * H:2 * B + (k + 1) * H, :])
    load(root_ref, x_ref)

    rows_at = lax.broadcasted_iota(jnp.int32, (H, H), 0)
    cols_at = lax.broadcasted_iota(jnp.int32, (H, H), 1)
    corner = (rows_at == 0) & (cols_at == H - 1)
    for copy_in in loads:
        copy_in.wait()
    for at, slot, par in ((0, top_slot, lambda k: tpar[0, k]), (1, sub_slot, lambda k: spar[0, 0, k])):
        for k in range(2):
            quarter = jnp.where(corner, par(k).astype(F32), corners[at, k].astype(F32))
            slots[slot, 3 * B:3 * B + H, k * H:(k + 1) * H] = quarter.astype(BF16)

    pl.semaphore_wait(barrier, 7)

    def copy(src, dst, k, sid, where, chunks=CH):
        size = ROWS // chunks
        rows = pl.ds(pl.multiple_of(k * size, size), size)
        return pltpu.make_async_remote_copy(
            src_ref=slots.at[src, rows, :], dst_ref=slots.at[dst, rows, :],
            send_sem=send_sem.at[sid], recv_sem=recv_sem.at[dst, k],
            device_id=where, device_id_type=MESH)

    def arrived(slot, k, chunks=CH):
        copy(slot, slot, k, 0, other, chunks).wait_recv()

    up2 = (z >= 2) & (z <= 6)
    zflows = (
        (T0, jnp.where(z < 4, z, 8 - z), z >= 0, 0, ZCH, z >= 1,
         ((S_T0P, zp, z < 3, 0, ZCH), (S_T0M, zm, (z == 0) | (z > 4), 0, ZCH))),
        (T1, pick((1, 0, 1, 2, 3, 4, 0, 2), z), z != 6, 0, ZCH, (z == 3) | (z == 5) | (z == 7),
         ((S_T1, zp, (z >= 1) & (z <= 4), 0, ZCH), (S_T1M, zm, z <= 1, 0, ZCH))),
        (T2, jnp.where(up2, z - 2, (10 - z) % 8), z >= 0,
         jnp.where(up2, 0, ZUP), jnp.where((z >= 3) & (z <= 5), ZUP, ZCH), z == 6,
         ((S_T2, zp, (z >= 2) & (z <= 5), 0, ZUP), (S_T2M, zm, (z <= 2) | (z == 7), ZUP, ZCH))),
        (T3, z - 3, z >= 3, 0, ZCH, z == 7, ((S_T3, zp, z < 7, 0, ZCH),)),
    )
    rx_depth = pick((0, 1, 2, 1), x)
    y0_depth = rx_depth + pick((0, 1, 2, 1), y)
    y1_depth = rx_depth + y - 1
    d0_depth = jnp.where(y == 0, rx_depth, y0_depth) + 1

    pflows = (
        (RX, rx_depth, x >= 0, (
            (RX, S_XA, xp, x == 0), (RX, S_XB, xm, (x == 0) | (x == 3)),
            (Y0, S_YA, yp, y == 0), (Y0, S_YB, ym, y == 0),
            (Y1, S_Y1, yp, y == 1), (D0, S_DD, other, (c == 0) & (y == 0)))),
        (R1, x - 1, x >= 1, ((R1, S_R1, xp, x < 3),)),
        (Y0, y0_depth, y >= 1, (
            (Y0, S_YB, ym, y == 3), (D0, S_DD, other, c == 0))),
        (Y1, y1_depth, y >= 2, ((Y1, S_Y1, yp, y == 2),)),
    )

    def either(flags):
        return functools.reduce(jnp.logical_or, flags)

    def source(k, carry):
        for slot, depth, member, first, end, needed, outs in zflows:
            for sid, where, when, lo, hi in outs:
                @pl.when(member & (depth == 0) & when & (k >= lo) & (k < hi))
                def _():
                    copy(slot, slot, c * ZCH + k, sid, where, 2 * ZCH).start()
        for slot, depth, member, outs in pflows[:2]:
            for dst, sid, where, when in outs:
                @pl.when(member & (depth == 0) & when & (k < CH))
                def _():
                    copy(slot, dst, k, sid, where).start()
        return carry

    lax.fori_loop(0, max(CH, ZCH), source, 0)

    tri = rows_at >= cols_at

    after = lambda depth: ZHOP * depth + ZSTEP * ZCH
    plan = (
        (TOWN, z >= 4, 0, 0),
        (OWN, x >= 2, 0, 0),
        (T0, z >= 0, jnp.where(z > 0, after(zflows[0][1]), 0), jnp.where(z > 0, ZCH, 0)),
        (T1, z % 2 == 1, jnp.where(z > 1, after(zflows[1][1]), 0), jnp.where(z > 1, ZCH, 0)),
        (T2, z % 4 == 2, jnp.where(z > 2, after(zflows[2][1]), 0), jnp.where(z > 2, ZCH, 0)),
        (T3, z % 4 == 3, jnp.where(z > 3, after(zflows[3][1]), 0), jnp.where(z > 3, ZCH, 0)),
        (RX, x >= 0, jnp.where(x > 0, rx_depth + CH, 0),
         jnp.where((y >= 2) & ((x == 1) | (x == 2)), CH, 0)),
        (R1, x % 2 == 1, jnp.where(x > 1, x - 1 + CH, 0), jnp.where(x == 3, CH, 0)),
        (Y0, y >= 1, y0_depth + CH, jnp.where((y < 3) & (c == 1), CH, 0)),
        (Y1, y == 3, y1_depth + CH, CH),
        (D0, c == 1, d0_depth + CH, CH),
    )
    prep_ready, latest = [], jnp.int32(0)
    at_slot = {}
    for slot, needed, when, count in plan:
        latest = jnp.where(needed, jnp.maximum(latest, when), latest)
        prep_ready.append(latest)
        at_slot[slot] = latest

    def prepare(at, carry):
        slot = pick([entry[0] for entry in plan], at)

        @pl.when(pick([entry[1].astype(jnp.int32) for entry in plan], at) == 1)
        def _():
            def await_half(k, carry):
                arrived(slot, (1 - c) * ZCH + k, 2 * ZCH)
                return carry

            def await_chunk(k, carry):
                arrived(slot, k)
                return carry

            count = pick([entry[3] for entry in plan], at)
            lax.fori_loop(0, jnp.where(slot <= TOWN, count, 0), await_half, 0)
            lax.fori_loop(0, jnp.where(slot <= TOWN, 0, count), await_chunk, 0)
            for k in range(2):
                panel = slots[slot, k * B:(k + 1) * B, :]
                low = slots[slot, 2 * B + k * H:2 * B + (k + 1) * H, :]
                quarter = slots[slot, 3 * B:3 * B + H, k * H:(k + 1) * H].astype(F32)
                quarter = jnp.where(tri, quarter, 0.0).astype(BF16)
                v = jnp.concatenate(
                    [jnp.concatenate([quarter, jnp.zeros((H, H), BF16)], axis=1), low], axis=0)
                own_ref[slot, k] = lax.dot_general(
                    v, v, (((0,), (0,)), ((), ())), preferred_element_type=F32)
                carried = jnp.dot(panel, v, preferred_element_type=F32)
                ch, cl = split(carried)
                th, tl = split(carried.T)
                left_ref[slot, k] = jnp.concatenate([th, tl, th], axis=1)
                right_ref[slot, k] = jnp.concatenate([ch, ch, cl], axis=0)
        return carry

    chain_slot = (T0, T1, 2 + z % 2, TOWN, D0, jnp.where(y == 0, RX, Y0), Y1, RX, R1,
                  jnp.where(x == 1, R1, OWN))
    chain_on = (z >= 0, z % 2 == 1, (z // 2) % 2 == 1, z >= 4, c == 1, y >= 0, y == 3, y >= 1,
                x == 3, x >= 1)
    chain_at = (at_slot[T0], at_slot[T1], jnp.where(z % 2 == 0, at_slot[T2], at_slot[T3]), at_slot[TOWN],
                at_slot[D0], jnp.where(y == 0, at_slot[RX], at_slot[Y0]), at_slot[Y1], at_slot[RX],
                at_slot[R1], jnp.where(x == 1, at_slot[R1], at_slot[OWN]))
    ready, latest = [], jnp.int32(0)
    for s in range(10):
        latest = jnp.where(chain_on[s], jnp.maximum(latest, chain_at[s]), latest)
        ready.append(latest)

    def step(s, carry):
        slot = pick(chain_slot, s)

        @pl.when(pick([flag.astype(jnp.int32) for flag in chain_on], s) == 1)
        def _():
            above0, above1 = x_ref[0], x_ref[1]
            for k in range(2):
                quarter = slots[slot, 3 * B:3 * B + 16, k * H:(k + 1) * H].astype(F32)
                second = quarter[0:1, H - 1:H] > 0.5
                xh, xl = split(jnp.where(second, above1, above0))
                u = jnp.dot(left_ref[slot, k], jnp.concatenate([xh, xh, xl], axis=0),
                            preferred_element_type=F32)
                uh, ul = split(u)
                x_ref[k] = own_ref[slot, k] + jnp.dot(
                    jnp.concatenate([uh, ul, uh], axis=1), right_ref[slot, k],
                    preferred_element_type=F32)

        @pl.when(s == 3)
        def _():
            top_ref[0] = x_ref[...]
        return carry

    def relay(t, carry):
        prepared, done = carry

        for at, (slot, depth, member, first, end, needed, outs) in enumerate(zflows):
            late_by = t - ZHOP * depth
            j = late_by // ZSTEP

            @pl.when(member & (depth > 0) & (late_by % ZSTEP == 0) & (j >= first) & (j < end))
            def _():
                k = c * ZCH + j
                arrived(slot, k, 2 * ZCH)
                for sid, where, when, lo, hi in outs:
                    @pl.when(when)
                    def _():
                        copy(slot, slot, k, sid, where, 2 * ZCH).start()

                @pl.when(needed)
                def _():
                    copy(slot, slot, k, S_D0 + at, other, 2 * ZCH).start()

        for slot, depth, member, outs in pflows:
            k = t - depth

            @pl.when(member & (depth > 0) & (k >= 0) & (k < CH) & either([o[3] for o in outs]))
            def _():
                arrived(slot, k)
                for dst, sid, where, when in outs:
                    @pl.when(when)
                    def _():
                        copy(slot, dst, k, sid, where).start()

        def so_far(times):
            count = jnp.int32(0)
            for time in times:
                count += (time <= t).astype(jnp.int32)
            return count

        now = so_far(prep_ready)
        lax.fori_loop(prepared, now, prepare, 0)
        count = so_far(ready)
        count = jnp.where(t >= LAST, 10, jnp.minimum(count, done + PACE))
        lax.fori_loop(done, count, step, 0)
        return now, count

    lax.fori_loop(0, LAST + 1, relay, (jnp.int32(0), jnp.int32(0)))
    sub_ref[0, 0] = x_ref[...]

    def gone(sid, rows):
        part = slots.at[0, pl.ds(0, rows), :]
        pltpu.make_async_remote_copy(
            src_ref=part, dst_ref=part, send_sem=send_sem.at[sid], recv_sem=recv_sem.at[0, 0],
            device_id=other, device_id_type=MESH).wait_send()

    for at, (slot, depth, member, first, end, needed, outs) in enumerate(zflows):
        for sid, where, when, lo, hi in outs:
            @pl.when(member & when)
            def _():
                gone(sid, (hi - lo) * (ROWS // 2 // ZCH))

        @pl.when(needed & (depth > 0))
        def _():
            gone(S_D0 + at, ROWS // 2)

    streams = {}
    for slot, depth, member, outs in pflows:
        for dst, sid, where, when in outs:
            streams.setdefault(sid, []).append(member & when)
    for sid, flags in streams.items():
        @pl.when(either(flags))
        def _():
            gone(sid, ROWS)


def on_device(root_sigma, top_inv, top_panels, top_parents, sub_inv, sub_panels, sub_parents):
    vmem = pl.BlockSpec(memory_space=pltpu.VMEM)
    hbm = pl.BlockSpec(memory_space=pltpu.HBM)
    arrays = [pltpu.with_memory_space_constraint(a, pltpu.HBM) for a in
              (root_sigma, top_inv, top_panels, top_parents, sub_inv, sub_panels, sub_parents)]
    return pl.pallas_call(
        kernel,
        out_shape=(jax.ShapeDtypeStruct((1, 1, 2, B, B), F32),
                   jax.ShapeDtypeStruct((1, 2, B, B), F32)),
        in_specs=[hbm] * 7,
        out_specs=(vmem, vmem),
        scratch_shapes=[
            pltpu.VMEM((NSLOT, ROWS, B), BF16),
            pltpu.VMEM((2, B, B), F32),
            pltpu.VMEM((NSLOT, 2, B, B), F32),
            pltpu.VMEM((NSLOT, 2, B, 3 * B), BF16),
            pltpu.VMEM((NSLOT, 2, 3 * B, B), BF16),
            pltpu.VMEM((2, 2, H, H), BF16),
            pltpu.SMEM((1, 2), jnp.int32),
            pltpu.SMEM((1, 1, 2), jnp.int32),
            pltpu.SemaphoreType.DMA((15,)),
            pltpu.SemaphoreType.DMA((NSEND,)),
            pltpu.SemaphoreType.DMA((NSLOT, max(CH, 2 * ZCH))),
        ],
        compiler_params=pltpu.CompilerParams(
            collective_id=0, has_side_effects=True, vmem_limit_bytes=40 << 20),
    )(*arrays)


def solution(mesh):
    in_specs = (
        P(),
        P("leaf", None, None, None),
        P("leaf", None, None, None),
        P("leaf", None),
        P("leaf", "blk", None, None, None),
        P("leaf", "blk", None, None, None),
        P("leaf", "blk", None),
    )
    out_specs = (P("leaf", "blk", None, None, None), P("leaf", None, None, None))
    return jax.shard_map(
        on_device, mesh=mesh, in_specs=in_specs, out_specs=out_specs, check_vma=False
    )
```

time: 63.7 us -> 39.4 us (0.62)
  the two profiles are of different devices: /device:TPU:245 before, /device:TPU:181 now
where the time goes in v2:
time: 39.4 us; the launch traced here: 39.3 us
  Pallas kernels  37.1 us (94%)
  local copies, waits for them, and re-layouts  1.59 us (4%)
  between operations  0.64 us (2%)
    pallas_call x1, Pallas kernels, on_device(): pl.pallas_call(kernel, out_shape=(jax.ShapeDtypeStruct((1, 1, 2, B, B), F...  37.1 us
    unnamed x2, local copies, waits for them, and re-layouts  1.59 us

profile of v2, /device:TPU:181, one launch (start us, length us, event | category | flops | bytes accessed | tf_op | source)
XLA Modules:
  0.0 39.3 jit_solution(5348980765112187593)
XLA Ops:
  0.6 37.1 %shard_map.86 = (f32[1,1,2,256,256]{4,3,2,1,0:T(8,128)S(1)}, f32[1,2,256,256]{3,2,1,0:T(8,128)S(1)}) custom-call(f32[2,256,256]{2,1,0:T(8,128)} %root_ref.1, bf16[1,2,256,256]{3,2,1,0:T(8,128)(2,1)} %tinv_ref.1, bf16[1,2,256,256]{3,2,1,0:T(8,128)(2,1)} %tpan_ref.1, s32[1,2]{1,0:T(1,128)} %tpar_ref.1, bf16[1,1,2,256,256]{4,3,2,1,0:T(8,128)(2,1)} %sinv_ref.1, ...), custom_call_target="tpu_custom_call" | custom-call | tf_op jit(solution)/shard_map/pallas_call | solution.py:317
  37.7 0.8 %copy.11 = f32[1,1,2,256,256]{4,3,2,1,0:T(8,128)} copy(f32[1,1,2,256,256]{4,3,2,1,0:T(8,128)S(1)} %get-tuple-element.4) | data formatting | bytes 1048576
  38.5 0.8 %copy.12 = f32[1,2,256,256]{3,2,1,0:T(8,128)} copy(f32[1,2,256,256]{3,2,1,0:T(8,128)S(1)} %get-tuple-element.5) | data formatting | bytes 1048576

commit v3 on v2

--- a/solution.py
+++ b/solution.py
@@ -12,7 +12,8 @@
 BF16 = jnp.bfloat16
 B = 256
 H = 128
-ROWS = 896
+ROWS = 784
+ZROWS = 832
 CH = 7
 ZCH = 2
 PACE = 2
@@ -73,25 +74,34 @@
     for at, slot, inv, pan in ((0, top_slot, tinv_ref.at[0], tpan_ref.at[0]),
                                (1, sub_slot, sinv_ref.at[0, 0], span_ref.at[0, 0])):
         for k in range(2):
-            load(inv.at[k, 0:H, 0:H], corners.at[at, k])
+            load(inv.at[k, 0:H, 0:H], corners.at[at, k, 0])
+            load(inv.at[k, H:B, H:B], corners.at[at, k, 1])
             load(pan.at[k], slots.at[slot, k * B:(k + 1) * B, :])
-            load(inv.at[k, H:B, :], slots.at[slot, 2 * B + k * H:2 * B + (k + 1) * H, :])
+            load(inv.at[k, H:B, 0:H], slots.at[slot, 2 * B:2 * B + H, k * H:(k + 1) * H])
     load(root_ref, x_ref)
 
     rows_at = lax.broadcasted_iota(jnp.int32, (H, H), 0)
     cols_at = lax.broadcasted_iota(jnp.int32, (H, H), 1)
-    corner = (rows_at == 0) & (cols_at == H - 1)
+    tri = rows_at >= cols_at
+    above = rows_at < cols_at
+    even = rows_at == cols_at
+    tile_row = lax.broadcasted_iota(jnp.int32, (16, H), 0)
     for copy_in in loads:
         copy_in.wait()
     for at, slot, par in ((0, top_slot, lambda k: tpar[0, k]), (1, sub_slot, lambda k: spar[0, 0, k])):
         for k in range(2):
-            quarter = jnp.where(corner, par(k).astype(F32), corners[at, k].astype(F32))
-            slots[slot, 3 * B:3 * B + H, k * H:(k + 1) * H] = quarter.astype(BF16)
+            first, second = corners[at, k, 0].astype(F32), corners[at, k, 1].astype(F32)
+            folded = jnp.where(above, second.T, first)
+            slots[slot, 2 * B + H:3 * B, k * H:(k + 1) * H] = folded.astype(BF16)
+            diagonal = jnp.sum(jnp.where(even, second, 0.0), axis=0, keepdims=True)
+            tile = jnp.where(tile_row == 0, diagonal, par(k).astype(F32))
+            slots[slot, 3 * B:ROWS, k * H:(k + 1) * H] = tile.astype(BF16)
+    slots[top_slot, ROWS:ZROWS, :] = jnp.zeros((ZROWS - ROWS, B), BF16)
 
     pl.semaphore_wait(barrier, 7)
 
     def copy(src, dst, k, sid, where, chunks=CH):
-        size = ROWS // chunks
+        size = (ROWS if chunks == CH else ZROWS) // chunks
         rows = pl.ds(pl.multiple_of(k * size, size), size)
         return pltpu.make_async_remote_copy(
             src_ref=slots.at[src, rows, :], dst_ref=slots.at[dst, rows, :],
@@ -145,8 +155,6 @@
         return carry
 
     lax.fori_loop(0, max(CH, ZCH), source, 0)
-
-    tri = rows_at >= cols_at
 
     after = lambda depth: ZHOP * depth + ZSTEP * ZCH
     plan = (
@@ -188,11 +196,14 @@
             lax.fori_loop(0, jnp.where(slot <= TOWN, 0, count), await_chunk, 0)
             for k in range(2):
                 panel = slots[slot, k * B:(k + 1) * B, :]
-                low = slots[slot, 2 * B + k * H:2 * B + (k + 1) * H, :]
-                quarter = slots[slot, 3 * B:3 * B + H, k * H:(k + 1) * H].astype(F32)
-                quarter = jnp.where(tri, quarter, 0.0).astype(BF16)
+                left = slots[slot, 2 * B:2 * B + H, k * H:(k + 1) * H]
+                folded = slots[slot, 2 * B + H:3 * B, k * H:(k + 1) * H].astype(F32)
+                diagonal = slots[slot, 3 * B:ROWS, k * H:(k + 1) * H].astype(F32)[0:1, :]
+                first = jnp.where(tri, folded, 0.0).astype(BF16)
+                second = jnp.where(even, diagonal, jnp.where(above, 0.0, folded.T)).astype(BF16)
                 v = jnp.concatenate(
-                    [jnp.concatenate([quarter, jnp.zeros((H, H), BF16)], axis=1), low], axis=0)
+                    [jnp.concatenate([first, jnp.zeros((H, H), BF16)], axis=1),
+                     jnp.concatenate([left, second], axis=1)], axis=0)
                 own_ref[slot, k] = lax.dot_general(
                     v, v, (((0,), (0,)), ((), ())), preferred_element_type=F32)
                 carried = jnp.dot(panel, v, preferred_element_type=F32)
@@ -221,8 +232,8 @@
         def _():
             above0, above1 = x_ref[0], x_ref[1]
             for k in range(2):
-                quarter = slots[slot, 3 * B:3 * B + 16, k * H:(k + 1) * H].astype(F32)
-                second = quarter[0:1, H - 1:H] > 0.5
+                tile = slots[slot, 3 * B:ROWS, k * H:(k + 1) * H].astype(F32)
+                second = tile[1:2, 0:1] > 0.5
                 xh, xl = split(jnp.where(second, above1, above0))
                 u = jnp.dot(left_ref[slot, k], jnp.concatenate([xh, xh, xl], axis=0),
                             preferred_element_type=F32)
@@ -293,11 +304,11 @@
         for sid, where, when, lo, hi in outs:
             @pl.when(member & when)
             def _():
-                gone(sid, (hi - lo) * (ROWS // 2 // ZCH))
+                gone(sid, (hi - lo) * (ZROWS // 2 // ZCH))
 
         @pl.when(needed & (depth > 0))
         def _():
-            gone(S_D0 + at, ROWS // 2)
+            gone(S_D0 + at, ZROWS // 2)
 
     streams = {}
     for slot, depth, member, outs in pflows:
@@ -321,15 +332,15 @@
         in_specs=[hbm] * 7,
         out_specs=(vmem, vmem),
         scratch_shapes=[
-            pltpu.VMEM((NSLOT, ROWS, B), BF16),
+            pltpu.VMEM((NSLOT, ZROWS, B), BF16),
             pltpu.VMEM((2, B, B), F32),
             pltpu.VMEM((NSLOT, 2, B, B), F32),
             pltpu.VMEM((NSLOT, 2, B, 3 * B), BF16),
             pltpu.VMEM((NSLOT, 2, 3 * B, B), BF16),
-            pltpu.VMEM((2, 2, H, H), BF16),
+            pltpu.VMEM((2, 2, 2, H, H), BF16),
             pltpu.SMEM((1, 2), jnp.int32),
             pltpu.SMEM((1, 1, 2), jnp.int32),
-            pltpu.SemaphoreType.DMA((15,)),
+            pltpu.SemaphoreType.DMA((19,)),
             pltpu.SemaphoreType.DMA((NSEND,)),
             pltpu.SemaphoreType.DMA((NSLOT, max(CH, 2 * ZCH))),
         ],

time: 39.4 us -> 38.4 us (0.975)
  Pallas kernels: 37.1 us -> 36.1 us
    pallas_call x1, Pallas kernels: 37.1 us -> 36.1 us  [on_device(): pl.pallas_call(kernel, out_shape=(jax.ShapeDtypeStruct((1, 1, 2, B, B), F...]
where the time goes in v3:
time: 38.4 us; the launch traced here: 38.3 us
  Pallas kernels  36.1 us (94%)
  local copies, waits for them, and re-layouts  1.59 us (4%)
  between operations  0.64 us (2%)
    pallas_call x1, Pallas kernels, on_device(): pl.pallas_call(kernel, out_shape=(jax.ShapeDtypeStruct((1, 1, 2, B, B), F...  36.1 us
    unnamed x2, local copies, waits for them, and re-layouts  1.59 us

profile of v3, /device:TPU:181, one launch (start us, length us, event | category | flops | bytes accessed | tf_op | source)
XLA Modules:
  0.0 38.3 jit_solution(15865734650469157735)
XLA Ops:
  0.6 36.1 %shard_map.86 = (f32[1,1,2,256,256]{4,3,2,1,0:T(8,128)S(1)}, f32[1,2,256,256]{3,2,1,0:T(8,128)S(1)}) custom-call(f32[2,256,256]{2,1,0:T(8,128)} %root_ref.1, bf16[1,2,256,256]{3,2,1,0:T(8,128)(2,1)} %tinv_ref.1, bf16[1,2,256,256]{3,2,1,0:T(8,128)(2,1)} %tpan_ref.1, s32[1,2]{1,0:T(1,128)} %tpar_ref.1, bf16[1,1,2,256,256]{4,3,2,1,0:T(8,128)(2,1)} %sinv_ref.1, ...), custom_call_target="tpu_custom_call" | custom-call | tf_op jit(solution)/shard_map/pallas_call | solution.py:328
  36.7 0.8 %copy.11 = f32[1,1,2,256,256]{4,3,2,1,0:T(8,128)} copy(f32[1,1,2,256,256]{4,3,2,1,0:T(8,128)S(1)} %get-tuple-element.4) | data formatting | bytes 1048576
  37.5 0.8 %copy.12 = f32[1,2,256,256]{3,2,1,0:T(8,128)} copy(f32[1,2,256,256]{3,2,1,0:T(8,128)S(1)} %get-tuple-element.5) | data formatting | bytes 1048576
